TPU v7x, 32 devices: a whole 2x2x4 slice. The times are simulated.
32 devices in a mesh: dom: 8 (over z, y), wa: 4 (over x, core).
Axes of the slice: x: 2, y: 2, z: 4, core: 2. Of those that a mesh axis runs over, the one named last changes fastest.
Arguments:
- bond_feats: bfloat16 [2048, 256], P('dom'), may hold values from -6 to 6
- cotangent: bfloat16 [2048, 256], P('dom', 'wa'), may hold values from -6 to 6
- bond_count: int32 [8], P('dom'), may hold values from 128 to 256, as said below
- source: int32 [24576], P('dom'), may hold values from 0 to 319, as said below
- cosine: float32 [24576], P('dom'), may hold values from -1 to 1
- w_source: bfloat16 [256, 256], P(None, 'wa'), may hold values from -0.375 to 0.375
- w_target: bfloat16 [256, 256], P(None, 'wa'), may hold values from -0.375 to 0.375
- w_message: bfloat16 [256, 256], P(None, 'wa'), may hold values from -0.375 to 0.375
- w_self: bfloat16 [256, 256], P(None, 'wa'), may hold values from -0.375 to 0.375
- gate_angle: float32 [256], P('wa'), may hold values from -4 to 4
Outputs:
- bond_grad: bfloat16 [2048, 256], P('dom', 'wa')
- grad_source: float32 [256, 256], P('dom', 'wa')
- grad_target: float32 [256, 256], P('dom', 'wa')
- grad_message: float32 [256, 256], P('dom', 'wa')
- grad_self: float32 [256, 256], P('dom', 'wa')
- grad_gate: float32 [256], P('wa')
Inputs may be any that keep to these rules, and one draw needn't show every extreme that they name: `bond_count`: every domain has 128 or more live bonds; some domain has all 256 live. `source`: each angle's other bond is a live row of the extended block of its domain: a ghost row (below 32 or at 288 or above) or 32 plus a live own row.
All inputs are finite; a program needn't handle non-finite values.
Results may differ from a plain program's by a relative error of at most 0.0085.
Values may be sent and summed in bfloat16 or wider, within the bound.
A program may use at most 64 MiB of HBM per device.

v0:
```python
import jax
import jax.numpy as jnp
from jax import lax
from jax.sharding import PartitionSpec as P

ARITY = 12
GHOST = 32


epsilon = 1e-06


def padded(block, sides, width):
    for axis, dim in sides:
        count = lax.axis_size(axis)
        forward = [(i, i + 1) for i in range(count - 1)]
        forward.append((count - 1, 0))
        backward = [(target, source) for source, target in forward]
        low = lax.ppermute(
            lax.slice_in_dim(block, block.shape[dim] - width, None, axis=dim), axis, forward
        )
        high = lax.ppermute(lax.slice_in_dim(block, 0, width, axis=dim), axis, backward)
        block = jnp.concatenate([low, block, high], axis=dim)
    return block


def shifted(block, axis, distance):
    devices = range(lax.axis_size(axis))
    route = [((i - distance) % len(devices), i) for i in devices]
    return lax.ppermute(block, axis, route)


def silu_slope(values):
    sigma = jax.nn.sigmoid(values)
    return sigma * (1.0 + values * (1.0 - sigma))


def per_device(
    bond_feats,
    cotangent,
    bond_count,
    source,
    cosine,
    w_source,
    w_target,
    w_message,
    w_self,
    gate_angle,
):
    capacity = bond_feats.shape[0]
    ext_rows = capacity + 2 * GHOST
    extended = padded(bond_feats, (("dom", 0),), GHOST)

    def spread(values):
        return jnp.broadcast_to(values[:, None, :], (capacity, ARITY, values.shape[1])).reshape(
            ARITY * capacity, values.shape[1]
        )

    def per_bond(values):
        return values.reshape(capacity, ARITY, values.shape[1]).sum(axis=1)

    rows = jnp.arange(capacity, dtype=jnp.int32)
    count = bond_count[0]
    live = ((rows < count - GHOST) | (rows >= capacity - GHOST)).astype(jnp.float32)
    alive = jnp.broadcast_to(live[:, None], (capacity, ARITY)).reshape(ARITY * capacity)[:, None]
    proj_source = jnp.dot(extended, w_source, preferred_element_type=jnp.float32)
    proj_message = jnp.dot(extended, w_message, preferred_element_type=jnp.float32)
    proj_target = jnp.dot(bond_feats, w_target, preferred_element_type=jnp.float32)
    base = jnp.dot(bond_feats, w_self, preferred_element_type=jnp.float32)
    picked_source = jnp.take(proj_source, source, axis=0)
    picked_message = jnp.take(proj_message, source, axis=0)
    pre = picked_source + spread(proj_target) + cosine[:, None] * gate_angle[None, :]
    sigma = jax.nn.sigmoid(pre)
    gated = sigma * alive
    numer = per_bond(gated * picked_message)
    denom = per_bond(gated) + epsilon
    aggregate = numer / denom
    hidden = base + aggregate
    cot_live = cotangent.astype(jnp.float32) * live[:, None]
    dhidden = cot_live * silu_slope(hidden)
    dnumer = dhidden / denom
    ddenom = -dhidden * aggregate / denom
    dgate = spread(dnumer) * picked_message + spread(ddenom)
    dmessage = gated * spread(dnumer)
    dpre = dgate * sigma * (1.0 - sigma) * alive
    dsource = jax.ops.segment_sum(dpre, source, num_segments=ext_rows)
    dmsg_rows = jax.ops.segment_sum(dmessage, source, num_segments=ext_rows)
    dtarget = per_bond(dpre)
    gate_term = jnp.sum(cosine[:, None] * dpre, axis=0)
    round_source = dsource.astype(jnp.bfloat16)
    round_message = dmsg_rows.astype(jnp.bfloat16)
    round_target = dtarget.astype(jnp.bfloat16)
    round_hidden = dhidden.astype(jnp.bfloat16)
    grad_one = jnp.dot(extended.T, round_source, preferred_element_type=jnp.float32)
    grad_two = jnp.dot(bond_feats.T, round_target, preferred_element_type=jnp.float32)
    grad_four = jnp.dot(extended.T, round_message, preferred_element_type=jnp.float32)
    grad_five = jnp.dot(bond_feats.T, round_hidden, preferred_element_type=jnp.float32)
    dext = jnp.dot(round_source, w_source.T, preferred_element_type=jnp.float32) + jnp.dot(
        round_message, w_message.T, preferred_element_type=jnp.float32
    )
    down = jnp.dot(round_target, w_target.T, preferred_element_type=jnp.float32) + jnp.dot(
        round_hidden, w_self.T, preferred_element_type=jnp.float32
    )
    whole = dext.at[GHOST : GHOST + capacity].add(down)
    summed = lax.psum_scatter(
        whole.astype(jnp.bfloat16), "wa", scatter_dimension=1, tiled=True
    ).astype(jnp.float32)
    own_part = summed[GHOST : GHOST + capacity]
    next_part = shifted(summed[:GHOST], "dom", -1)
    prev_part = shifted(summed[GHOST + capacity :], "dom", 1)
    own_part = own_part.at[capacity - GHOST :].add(next_part)
    own_part = own_part.at[:GHOST].add(prev_part)
    bond_grad = (own_part + cot_live).astype(jnp.bfloat16)
    sums_one, sums_two, sums_four, sums_five = (
        lax.psum_scatter(grad_one, "dom", scatter_dimension=0, tiled=True),
        lax.psum_scatter(grad_two, "dom", scatter_dimension=0, tiled=True),
        lax.psum_scatter(grad_four, "dom", scatter_dimension=0, tiled=True),
        lax.psum_scatter(grad_five, "dom", scatter_dimension=0, tiled=True),
    )
    grad_gate = lax.psum(gate_term, "dom")
    return (bond_grad, sums_one, sums_two, sums_four, sums_five, grad_gate)


def solution(mesh):
    return jax.shard_map(
        per_device,
        mesh=mesh,
        in_specs=(
            P("dom", None),
            P("dom", "wa"),
            P("dom"),
            P("dom"),
            P("dom"),
            P(None, "wa"),
            P(None, "wa"),
            P(None, "wa"),
            P(None, "wa"),
            P("wa"),
        ),
        out_specs=(
            P("dom", "wa"),
            P("dom", "wa"),
            P("dom", "wa"),
            P("dom", "wa"),
            P("dom", "wa"),
            P("wa"),
        ),
        check_vma=False,
    )
```

profile of v0, /device:TPU:0, one launch (start us, length us, event | category | flops | bytes accessed | tf_op | source)
XLA Modules:
  0.0 399.0 jit_solution(1793232076520562783)
XLA Ops:
  8.0 3.0 collective-permute-start
  11.0 3.0 collective-permute-start.1
  19.5 1.6 reshape.124
  22.1 9.6 %gather_fusion = f32[3072,64]{1,0:T(8,128)S(1)} fusion(f32[320,64]{1,0:T(8,128)S(1)} %fusion.27, s32[3072]{0:T(1024)} %fusion.24), kind=kCustom, calls=%fused_computation.clone | custom fusion | bytes 1585152 | tf_op jit(solution)/shard_map/jit(_take)/gather | solution.py:70
  31.7 12.0 %gather_fusion.1 = f32[3072,64]{1,0:T(8,128)} fusion(f32[320,64]{1,0:T(8,128)S(1)} %fusion.29, s32[3072]{0:T(1024)} %fusion.24), kind=kCustom, calls=%fused_computation.1.clone | custom fusion | bytes 1585152 | tf_op jit(solution)/shard_map/jit(_take)/gather | solution.py:71
  43.7 5.1 %select_multiply_fusion = (f32[3072,64]{1,0:T(8,128)}, f32[3072,64]{1,0:T(8,128)}) fusion(f32[3072,64]{1,0:T(8,128)} %gather_fusion.1, pred[3072]{0:T(1024)(128)(4,1)S(1)} %compare_and_fusion, f32[3072]{0:T(1024)S(1)} %mul.75, f32[64]{0:T(128)S(1)} %copy-done.19, f32[3072]{0:T(1024)S(1)} %copy-done.13, f32[3072,64]{1,0:T(8,128)S(1)} %reshape.124, ...), kind=kLoop, calls=%fused_computation.14 | loop fusion | flops 1966080 | bytes 3960064 | tf_op jit(solution)/shard_map/mul | solution.py:75
  48.8 2.6 reshape.126
  51.4 2.2 reduce_sum.37
  55.1 2.1 reduce_sum.36
  59.8 1.6 reshape.127
  63.8 2.5 reshape.128
  66.3 5.9 %multiply_reduce_fusion = (f32[64]{0:T(128)}, f32[3072,64]{1,0:T(8,128)}) fusion(f32[3072]{0:T(1024)S(1)} %copy-done.13, f32[3072]{0:T(1024)S(1)} %mul.75, f32[64]{0:T(128)S(1)} %copy-done.19, f32[3072,64]{1,0:T(8,128)S(1)} %reshape.124, f32[3072,64]{1,0:T(8,128)} %copy-done.1, f32[3072,64]{1,0:T(8,128)} %reshape.128, f32[3072,64]{1,0:T(8,128)S(1)} %reshape.127, ...), kind=kLoop, calls=%fused_computation.10 | loop fusion | flops 3145664 | bytes 4746752 | tf_op jit(solution)/shard_map/reduce_sum | solution.py:89
  72.2 2.7 reshape.129
  74.9 17.9 %scatter_custom_fusion = f32[320,64]{1,0:T(8,128)} fusion(s32[3072]{0:T(1024)} %param.21, f32[3072,64]{1,0:T(8,128)} %get-tuple-element.74, f32[]{:T(128)} %constant.100.clone.1), kind=kCustom, calls=%fused_computation.24 | custom fusion | flops 196608 | bytes 82432 | tf_op jit(solution)/shard_map/scatter-add | solution.py:86
  92.8 17.2 %scatter_custom_fusion.1 = f32[320,64]{1,0:T(8,128)S(1)} fusion(s32[3072]{0:T(1024)} %param.21, f32[3072,64]{1,0:T(8,128)S(1)} %copy-done.2, f32[3072,64]{1,0:T(8,128)S(1)} %reshape.127, f32[]{:T(128)} %constant.100.clone.1), kind=kCustom, calls=%fused_computation.11 | custom fusion | flops 393216 | bytes 1655296 | tf_op jit(solution)/shard_map/scatter-add | solution.py:87
  110.0 2.1 reduce_sum.38
  116.8 15.6 %reduce-scatter.16.cloned.1.call-done = bf16[64,320]{1,0:T(8,128)(2,1)} async-done(((bf16[256,320]{1,0:T(8,128)(2,1)}), bf16[64,320]{1,0:T(8,128)(2,1)}) %reduce-scatter.16.cloned.1.call-update) | async-done | bytes 40976
  133.4 4.2 %collective-permute-start.2 = (f32[32,64]{0,1:T(8,128)S(1)}, f32[32,64]{0,1:T(8,128)S(1)}, u32[]{:S(2)}, u32[]{:S(2)}) collective-permute-start(f32[32,64]{0,1:T(8,128)S(1)} %get-tuple-element.82), channel_id=1, source_target_pairs={{4,0},{8,4},{12,8},{16,12},{20,16},{24,20},{28,24},{0,28},{5,1},{9... | collective-permute-start | bytes 24584 | tf_op jit(solution)/shard_map/ppermute | solution.py:30
  138.5 18.2 %psum.7 = f32[64]{0:T(128)} all-reduce(f32[64]{0:T(128)S(1)} %copy-done.20), channel_id=1, replica_groups=mesh['dom'=8,'wa'=4] {'dom'}, use_global_device_ids=true, to_apply=%region_11.13 | all-reduce | flops 64 | bytes 512 | tf_op jit(solution)/shard_map/psum | solution.py:120
  158.7 4.7 %collective-permute-done.3 = f32[32,64]{0,1:T(8,128)S(1)} collective-permute-done((f32[32,64]{0,1:T(8,128)S(1)}, f32[32,64]{0,1:T(8,128)S(1)}, u32[]{:S(2)}, u32[]{:S(2)}) %collective-permute-start.3) | collective-permute-done | bytes 8224 | tf_op jit(solution)/shard_map/ppermute | solution.py:30
  164.5 33.8 %reduce-scatter.18.cloned.1.call-done = f32[32,64]{1,0:T(8,128)} async-done(((f32[256,64]{1,0:T(8,128)}), f32[32,64]{1,0:T(8,128)}) %reduce-scatter.18.cloned.1.call-update) | async-done | bytes 8208
  198.3 64.8 %reduce-scatter.12.cloned.1.call-done = f32[32,64]{1,0:T(8,128)} async-done(((f32[256,64]{1,0:T(8,128)}), f32[32,64]{1,0:T(8,128)}) %reduce-scatter.12.cloned.1.call-update) | async-done | bytes 8208 | tf_op jit(solution)/shard_map/reduce_scatter | solution.py:115
  263.2 64.7 %reduce-scatter.14.cloned.1.call-done = f32[32,64]{1,0:T(8,128)} async-done(((f32[256,64]{1,0:T(8,128)}), f32[32,64]{1,0:T(8,128)}) %reduce-scatter.14.cloned.1.call-update) | async-done | bytes 8208 | tf_op jit(solution)/shard_map/reduce_scatter | solution.py:117
  327.9 64.6 %reduce-scatter.20.cloned.1.call-done = f32[32,64]{1,0:T(8,128)} async-done(((f32[256,64]{1,0:T(8,128)}), f32[32,64]{1,0:T(8,128)}) %reduce-scatter.20.cloned.1.call-update) | async-done | bytes 8208
  (97 shorter events, 22.4 us)
Async XLA Ops:
  7.2 50.1 %copy-start = (bf16[256,64]{0,1:T(8,128)(2,1)S(1)}, bf16[256,64]{0,1:T(8,128)(2,1)}, u32[]{:S(2)}) copy-start(bf16[256,64]{0,1:T(8,128)(2,1)} %param.26) | copy-start | bytes 98308
  7.2 125.3 %reduce-scatter.16.cloned.1.call-start = ((), (), s32[]{:S(2)}) async-start(), calls=%async_computation.7 | async-start | bytes 245760
  8.0 13.2 %collective-permute-start = (bf16[32,256]{1,0:T(8,128)(2,1)S(1)}, bf16[32,256]{1,0:T(8,128)(2,1)S(1)}, u32[]{:S(2)}, u32[]{:S(2)}) collective-permute-start(bf16[32,256]{1,0:T(8,128)(2,1)S(1)} %get-tuple-element.80), channel_id=1, source_target_pairs={{0,4},{4,8},{8,12},{12,16},{16,20},{20,24},{24,28},{28,0},{1,5},{5... | collective-permute-start | bytes 49160 | tf_op jit(solution)/shard_map/ppermute | solution.py:19
  11.0 10.2 %collective-permute-start.1 = (bf16[32,256]{1,0:T(8,128)(2,1)S(1)}, bf16[32,256]{1,0:T(8,128)(2,1)S(1)}, u32[]{:S(2)}, u32[]{:S(2)}) collective-permute-start(bf16[32,256]{1,0:T(8,128)(2,1)S(1)} %get-tuple-element.79), channel_id=1, source_target_pairs={{4,0},{8,4},{12,8},{16,12},{20,16},{24,20},{28,24},{0,28},{5,1},{9... | collective-permute-start | bytes 49160 | tf_op jit(solution)/shard_map/ppermute | solution.py:22
  17.8 3.4 copy-start.16
  19.5 2.4 copy-start.11
  31.7 12.0 %copy-start.1 = (f32[3072,64]{1,0:T(8,128)}, f32[3072,64]{1,0:T(8,128)S(1)}, u32[]{:S(2)}) copy-start(f32[3072,64]{1,0:T(8,128)S(1)} %gather_fusion) | copy-start | bytes 2359300
  31.7 12.0 %copy-start.13 = (f32[3072]{0:T(1024)S(1)}, f32[3072]{0:T(1024)}, u32[]{:S(2)}) copy-start(f32[3072]{0:T(1024)} %param.22) | copy-start | bytes 36868
  31.7 12.0 %copy-start.19 = (f32[64]{0:T(128)S(1)}, f32[64]{0:T(128)}, u32[]{:S(2)}) copy-start(f32[64]{0:T(128)} %param.27) | copy-start | bytes 772
  51.4 2.2 copy-start.3
  55.1 2.2 copy-start.17
  72.2 20.6 %copy-start.2 = (f32[3072,64]{1,0:T(8,128)S(1)}, f32[3072,64]{1,0:T(8,128)}, u32[]{:S(2)}) copy-start(f32[3072,64]{1,0:T(8,128)} %get-tuple-element.76) | copy-start | bytes 2359300
  110.0 2.3 copy-start.8
  110.0 2.5 copy-start.12
  112.5 2.4 copy-start.5
  112.9 25.6 %copy-start.20 = (f32[64]{0:T(128)S(1)}, f32[64]{0:T(128)}, u32[]{:S(2)}) copy-start(f32[64]{0:T(128)} %get-tuple-element.73) | copy-start | bytes 772
  113.8 50.1 %copy-start.15 = (bf16[256,64]{0,1:T(8,128)(2,1)S(1)}, bf16[256,64]{0,1:T(8,128)(2,1)}, u32[]{:S(2)}) copy-start(bf16[256,64]{0,1:T(8,128)(2,1)} %param.19) | copy-start | bytes 98308
  113.8 50.1 %copy-start.18 = (f32[256]{0:T(256)S(1)}, f32[256]{0:T(256)}, u32[]{:S(2)}) copy-start(f32[256]{0:T(256)} %copy-done.16) | copy-start | bytes 3076
  113.8 84.5 %reduce-scatter.18.cloned.1.call-start = ((), (), s32[]{:S(2)}) async-start(), calls=%async_computation.8 | async-start | bytes 147456
  114.8 148.4 %reduce-scatter.12.cloned.1.call-start = ((), (), s32[]{:S(2)}) async-start(), calls=%async_computation.5 | async-start | bytes 147456 | tf_op jit(solution)/shard_map/reduce_scatter | solution.py:115
  115.8 212.1 %reduce-scatter.14.cloned.1.call-start = ((), (), s32[]{:S(2)}) async-start(), calls=%async_computation.6 | async-start | bytes 147456 | tf_op jit(solution)/shard_map/reduce_scatter | solution.py:117
  116.8 275.7 %reduce-scatter.20.cloned.1.call-start = ((), (), s32[]{:S(2)}) async-start(), calls=%async_computation.9 | async-start | bytes 147456
  133.4 24.9 %collective-permute-start.2 = (f32[32,64]{0,1:T(8,128)S(1)}, f32[32,64]{0,1:T(8,128)S(1)}, u32[]{:S(2)}, u32[]{:S(2)}) collective-permute-start(f32[32,64]{0,1:T(8,128)S(1)} %get-tuple-element.82), channel_id=1, source_target_pairs={{4,0},{8,4},{12,8},{16,12},{20,16},{24,20},{28,24},{0,28},{5,1},{9... | collective-permute-start | bytes 24584 | tf_op jit(solution)/shard_map/ppermute | solution.py:30
  156.8 6.6 %collective-permute-start.3 = (f32[32,64]{0,1:T(8,128)S(1)}, f32[32,64]{0,1:T(8,128)S(1)}, u32[]{:S(2)}, u32[]{:S(2)}) collective-permute-start(f32[32,64]{0,1:T(8,128)S(1)} %get-tuple-element.81), channel_id=1, source_target_pairs={{28,0},{0,4},{4,8},{8,12},{12,16},{16,20},{20,24},{24,28},{29,1},{... | collective-permute-start | bytes 24584 | tf_op jit(solution)/shard_map/ppermute | solution.py:30
  (6 other events, 10.6 us)
Sparse Core Ops, SparseCore 0:
  113.9 18.5 reduce-scatter.15
  136.4 61.9 reduce-scatter.17
  202.2 60.8 reduce-scatter.11
  266.9 60.9 reduce-scatter.13
  331.6 60.8 reduce-scatter.19
where the time goes:
time: 400 us; the launch traced here: 399 us
  waiting for transfers between devices  248 us (62%)
  other arithmetic  55.8 us (14%)
  local copies, waits for them, and re-layouts  44.7 us (11%)
  blocking collectives  18.2 us (5%)
  between operations  14.9 us (4%)
  starting transfers between devices  12 us (3%)
  matrix products  5.11 us (1%)
    unnamed x8, waiting for transfers between devices  114 us
    reduce_scatter x1, waiting for transfers between devices, per_device(): lax.psum_scatter(grad_one, 'dom', scatter_dimension=0, tiled=True)  64.8 us
    reduce_scatter x1, waiting for transfers between devices, per_device(): lax.psum_scatter(grad_four, 'dom', scatter_dimension=0, tiled=True)  64.7 us
    psum x1, blocking collectives, per_device(): grad_gate = lax.psum(gate_term, 'dom')  18.2 us
    scatter-add x1, other arithmetic, per_device(): dsource = jax.ops.segment_sum(dpre, source, num_segments=ext_rows)  17.9 us
    scatter-add x1, other arithmetic, per_device(): dmsg_rows = jax.ops.segment_sum(dmessage, source, num_segments=ext_rows)  17.2 us
    gather x1, local copies, waits for them, and re-layouts, per_device(): picked_message = jnp.take(proj_message, source, axis=0)  12 us
    gather x1, local copies, waits for them, and re-layouts, per_device(): picked_source = jnp.take(proj_source, source, axis=0)  9.59 us
  transfers between devices with their start and end apart: 9, of which 6 were waited for; matrix products, arithmetic and copies ran while one was open for 3% of the time, Pallas kernels for 0%

commit v1 on v0

v1 whole, which is shorter than its diff:
```python
import functools

import jax
import jax.numpy as jnp
from jax import lax
from jax.experimental import pallas as pl
from jax.experimental.pallas import tpu as pltpu
from jax.sharding import PartitionSpec as P

ARITY = 12
GHOST = 32
MESH = pl.DeviceIdType.MESH
LANES = 128

epsilon = 1e-06

NT = (((1,), (1,)), ((), ()))


def dot(a, b):
    return jnp.dot(a, b, preferred_element_type=jnp.float32)


def dot_nt(a, b):
    return lax.dot_general(a, b, NT, preferred_element_type=jnp.float32)


def split(values):
    high = values.astype(jnp.bfloat16)
    low = (values - high.astype(jnp.float32)).astype(jnp.bfloat16)
    return high, low


def flipped(values):
    return values.astype(jnp.float32).T


def kernel(
    n_dom,
    n_wa,
    fused,
    h_ref,
    cot_ref,
    count_ref,
    src_ref,
    cos_ref,
    ws_ref,
    wt_ref,
    wm_ref,
    wf_ref,
    ga_ref,
    bond_out,
    *refs,
):
    if fused:
        (g1_out, g2_out, g4_out, g5_out, gg_out) = refs[:5]
        refs = refs[5:]
    else:
        (g_out, gg_out) = refs[:2]
        refs = refs[2:]
    (
        wcat,
        wcat_t,
        h_t,
        gh,
        hot,
        table,
        picked,
        sig_s,
        dcol,
        own_w,
        wbuf,
        wrecv,
        gsend,
        grecv2,
        halo_send,
        halo_recv,
        wsend_sem,
        wrecv_sem,
        nsend_sem,
        nrecv_sem,
    ) = refs[:20]
    if fused:
        g_full, gbuf, grecv, gsend_sem, grecv_sem = refs[20:]
    dom = lax.axis_index("dom")
    wa = lax.axis_index("wa")
    capacity, depth = h_ref.shape
    cols = cot_ref.shape[1]
    up = (lax.rem(dom + 1, n_dom), wa)
    down = (lax.rem(dom + n_dom - 1, n_dom), wa)
    doms = range(1, n_dom) if fused else (1, n_dom - 1)

    barrier = pltpu.get_barrier_semaphore()
    for k in doms:
        pl.semaphore_signal(
            barrier, inc=1, device_id=(lax.rem(dom + k, n_dom), wa), device_id_type=MESH
        )
    for k in range(1, n_wa):
        pl.semaphore_signal(
            barrier, inc=1, device_id=(dom, lax.rem(wa + k, n_wa)), device_id_type=MESH
        )
    weights = jnp.concatenate([ws_ref[...], wm_ref[...], wt_ref[...], wf_ref[...]], axis=1)
    wcat[...] = weights
    wcat_t[...] = flipped(weights).astype(jnp.bfloat16)
    pl.semaphore_wait(barrier, len(doms) + n_wa - 1)

    to_up = pltpu.make_async_remote_copy(
        src_ref=h_ref.at[pl.ds(capacity - GHOST, GHOST), :],
        dst_ref=gh.at[pl.ds(0, GHOST), :],
        send_sem=halo_send.at[0],
        recv_sem=halo_recv.at[0],
        device_id=up,
        device_id_type=MESH,
    )
    to_down = pltpu.make_async_remote_copy(
        src_ref=h_ref.at[pl.ds(0, GHOST), :],
        dst_ref=gh.at[pl.ds(GHOST, GHOST), :],
        send_sem=halo_send.at[1],
        recv_sem=halo_recv.at[1],
        device_id=down,
        device_id_type=MESH,
    )
    to_up.start()
    to_down.start()

    ext = capacity + 2 * GHOST
    row_id = lax.broadcasted_iota(jnp.int32, (ext, capacity), 0)
    for j in range(ARITY):
        s = src_ref[j : j + 1, :]
        s = jnp.where(
            s < GHOST, s + capacity, jnp.where(s < capacity + GHOST, s - GHOST, s)
        )
        hot[:, j * capacity : (j + 1) * capacity] = jnp.where(
            row_id == s, 1.0, 0.0
        ).astype(jnp.bfloat16)
    h_t[:, :capacity] = flipped(h_ref[...]).astype(jnp.bfloat16)
    proj = dot_nt(wcat_t[...], h_ref[...])
    lane = lax.broadcasted_iota(jnp.int32, (1, capacity), 1)
    count = count_ref[0]
    live = jnp.where(
        (lane < count - GHOST) | (lane >= capacity - GHOST), 1.0, 0.0
    ).astype(jnp.float32)
    cot_live = flipped(cot_ref[...]) * live
    angle = jnp.broadcast_to(ga_ref[...], (LANES, cols)).T
    high, low = split(proj[: 2 * cols])
    table[: 2 * cols, :capacity] = high
    table[2 * cols :, :capacity] = low

    to_up.wait()
    to_down.wait()
    proj_g = dot_nt(wcat_t[: 2 * cols, :], gh[...])
    high, low = split(proj_g)
    table[: 2 * cols, capacity:] = high
    table[2 * cols :, capacity:] = low
    h_t[:, capacity:] = flipped(gh[...]).astype(jnp.bfloat16)

    picked[...] = dot(table[...], hot[...])

    parts_z = []
    parts_t = []
    gate_sum = jnp.zeros((cols, LANES), jnp.float32)
    for half in range(capacity // LANES):
        at = half * LANES
        q2 = proj[2 * cols : 3 * cols, at : at + LANES]
        base = proj[3 * cols :, at : at + LANES]
        lv = live[:, at : at + LANES]
        numer = jnp.zeros((cols, LANES), jnp.float32)
        denom = jnp.zeros((cols, LANES), jnp.float32)
        for j in range(ARITY):
            here = pl.ds(j * capacity + at, LANES)
            p1 = picked[0:cols, here] + picked[2 * cols : 3 * cols, here]
            p4 = picked[cols : 2 * cols, here] + picked[3 * cols :, here]
            pre = p1 + q2 + cos_ref[j : j + 1, at : at + LANES] * angle
            sig = jax.nn.sigmoid(pre)
            sig_s[:, here] = sig
            picked[cols : 2 * cols, here] = p4
            numer = numer + sig * p4
            denom = denom + sig
        inverse = 1.0 / (denom * lv + epsilon)
        agg = numer * lv * inverse
        z = base + agg
        sz = jax.nn.sigmoid(z)
        dz = cot_live[:, at : at + LANES] * (sz * (1.0 + z * (1.0 - sz)))
        dnum = dz * inverse
        dq2 = jnp.zeros((cols, LANES), jnp.float32)
        for j in range(ARITY):
            here = pl.ds(j * capacity + at, LANES)
            sig = sig_s[:, here]
            dmsg = sig * dnum
            dpre = dmsg * (picked[cols : 2 * cols, here] - agg) * (1.0 - sig)
            dq2 = dq2 + dpre
            gate_sum = gate_sum + cos_ref[j : j + 1, at : at + LANES] * dpre
            dcol[:cols, here] = dpre.astype(jnp.bfloat16)
            dcol[cols:, here] = dmsg.astype(jnp.bfloat16)
        parts_z.append(dz.astype(jnp.bfloat16))
        parts_t.append(dq2.astype(jnp.bfloat16))

    rows = dot_nt(dcol[...], hot[...]).astype(jnp.bfloat16)
    dcat = jnp.concatenate(
        [
            rows[:, :capacity],
            jnp.concatenate(parts_t, axis=1),
            jnp.concatenate(parts_z, axis=1),
        ],
        axis=0,
    )
    dghost = rows[:, capacity:]

    whole = dot(wcat[...], dcat)
    whole_g = dot(wcat[:, : 2 * cols], dghost)
    whole_g = jnp.concatenate(
        [whole_g, jnp.zeros((depth, LANES - 2 * GHOST), jnp.float32)], axis=1
    )
    own_w[:, :capacity] = whole
    own_w[:, capacity:] = whole_g
    for c in range(n_wa):
        wbuf[c, :, :capacity] = whole[c * cols : (c + 1) * cols].astype(jnp.bfloat16)
        wbuf[c, :, capacity:] = whole_g[c * cols : (c + 1) * cols].astype(jnp.bfloat16)
    wcopies = []
    for k in range(1, n_wa):
        to = lax.rem(wa + k, n_wa)
        copy = pltpu.make_async_remote_copy(
            src_ref=wbuf.at[to],
            dst_ref=wrecv.at[k - 1],
            send_sem=wsend_sem.at[k - 1],
            recv_sem=wrecv_sem.at[k - 1],
            device_id=(dom, to),
            device_id_type=MESH,
        )
        copy.start()
        wcopies.append(copy)

    grads = dot_nt(h_t[:, :capacity], dcat)
    grads_g = dot_nt(h_t[:, capacity:], dghost)
    grads = jnp.concatenate([grads[:, : 2 * cols] + grads_g, grads[:, 2 * cols :]], axis=1)
    high, low = split(gate_sum)
    ones = jnp.ones((16, LANES), jnp.bfloat16)
    gate_row = dot_nt(ones, high) + dot_nt(ones, low)
    gcopies = []
    if fused:
        chunk = depth // n_dom
        g_full[...] = grads
        row16 = lax.broadcasted_iota(jnp.int32, (16, cols), 0)
        ghigh = gate_row.astype(jnp.bfloat16).astype(jnp.float32)
        gate_block = jnp.where(row16 == 0, ghigh, gate_row - ghigh)
        gate_block = jnp.concatenate(
            [gate_block, jnp.zeros((16, 4 * cols - cols), jnp.float32)], axis=1
        ).astype(jnp.bfloat16)
        for i in range(n_dom):
            gbuf[i, :chunk, :] = grads[i * chunk : (i + 1) * chunk].astype(jnp.bfloat16)
            gbuf[i, chunk:, :] = gate_block
        for k in range(1, n_dom):
            to = lax.rem(dom + k, n_dom)
            copy = pltpu.make_async_remote_copy(
                src_ref=gbuf.at[to],
                dst_ref=grecv.at[k - 1],
                send_sem=gsend_sem.at[k - 1],
                recv_sem=grecv_sem.at[k - 1],
                device_id=(to, wa),
                device_id_type=MESH,
            )
            copy.start()
            gcopies.append(copy)
    else:
        g_out[...] = grads
        gg_out[...] = gate_row[0:1]

    for copy in wcopies:
        copy.wait()
    mine = pl.ds(pl.multiple_of(wa * cols, cols), cols)
    total = own_w[mine, :]
    for k in range(n_wa - 1):
        total = total + wrecv[k].astype(jnp.float32)
    gsend[...] = total[:, capacity:]
    ncopies = []
    for i, to in enumerate((up, down)):
        copy = pltpu.make_async_remote_copy(
            src_ref=gsend,
            dst_ref=grecv2.at[i],
            send_sem=nsend_sem.at[i],
            recv_sem=nrecv_sem.at[i],
            device_id=to,
            device_id_type=MESH,
        )
        copy.start()
        ncopies.append(copy)

    own = total[:, :capacity] + cot_live
    if fused:
        for copy in gcopies:
            copy.wait()
        acc = g_full[pl.ds(pl.multiple_of(dom * chunk, chunk), chunk), :]
        gate = gate_row[0:1]
        for k in range(n_dom - 1):
            acc = acc + grecv[k, :chunk, :].astype(jnp.float32)
            pair = grecv[k, chunk:, :cols].astype(jnp.float32)
            gate = gate + pair[0:1] + pair[1:2]
        g1_out[...] = acc[:, :cols]
        g4_out[...] = acc[:, cols : 2 * cols]
        g2_out[...] = acc[:, 2 * cols : 3 * cols]
        g5_out[...] = acc[:, 3 * cols :]
        gg_out[...] = gate

    for copy in ncopies:
        copy.wait()
    lane_t = lax.broadcasted_iota(jnp.int32, (cols, LANES), 1)
    below = pltpu.roll(grecv2[0], LANES - GHOST, 1)
    above = pltpu.roll(grecv2[1], LANES - GHOST, 1)
    first = own[:, :LANES] + jnp.where(lane_t < GHOST, below, 0.0)
    last = own[:, capacity - LANES :] + jnp.where(lane_t >= LANES - GHOST, above, 0.0)
    result = jnp.concatenate([first, own[:, LANES : capacity - LANES], last], axis=1) if capacity > 2 * LANES else jnp.concatenate([first, last], axis=1)
    bond_out[...] = result.T.astype(jnp.bfloat16)


def per_device(
    n_dom,
    n_wa,
    bond_feats,
    cotangent,
    bond_count,
    source,
    cosine,
    w_source,
    w_target,
    w_message,
    w_self,
    gate_angle,
):
    capacity, depth = bond_feats.shape
    cols = cotangent.shape[1]
    angles = source.shape[0]
    ext = capacity + 2 * GHOST
    chunk = depth // n_dom
    fused = chunk % 16 == 0
    src = source.reshape(capacity, ARITY).T
    cos = cosine.reshape(capacity, ARITY).T
    f32, bf16 = jnp.float32, jnp.bfloat16
    vmem = pl.BlockSpec(memory_space=pltpu.VMEM)
    outs = [jax.ShapeDtypeStruct((capacity, cols), bf16)]
    if fused:
        outs += [jax.ShapeDtypeStruct((chunk, cols), f32)] * 4
    else:
        outs += [jax.ShapeDtypeStruct((depth, 4 * cols), f32)]
    outs += [jax.ShapeDtypeStruct((1, cols), f32)]
    dma = pltpu.SemaphoreType.DMA
    scratch = [
        pltpu.VMEM((depth, 4 * cols), bf16),
        pltpu.VMEM((4 * cols, depth), bf16),
        pltpu.VMEM((depth, ext), bf16),
        pltpu.VMEM((2 * GHOST, depth), bf16),
        pltpu.VMEM((ext, angles), bf16),
        pltpu.VMEM((4 * cols, ext), bf16),
        pltpu.VMEM((4 * cols, angles), f32),
        pltpu.VMEM((cols, angles), f32),
        pltpu.VMEM((2 * cols, angles), bf16),
        pltpu.VMEM((depth, capacity + LANES), f32),
        pltpu.VMEM((n_wa, cols, capacity + LANES), bf16),
        pltpu.VMEM((n_wa - 1, cols, capacity + LANES), bf16),
        pltpu.VMEM((cols, LANES), f32),
        pltpu.VMEM((2, cols, LANES), f32),
        dma((2,)),
        dma((2,)),
        dma((n_wa - 1,)),
        dma((n_wa - 1,)),
        dma((2,)),
        dma((2,)),
    ]
    if fused:
        scratch += [
            pltpu.VMEM((depth, 4 * cols), f32),
            pltpu.VMEM((n_dom, chunk + 16, 4 * cols), bf16),
            pltpu.VMEM((n_dom - 1, chunk + 16, 4 * cols), bf16),
            dma((n_dom - 1,)),
            dma((n_dom - 1,)),
        ]
    results = pl.pallas_call(
        functools.partial(kernel, n_dom, n_wa, fused),
        out_shape=outs,
        in_specs=[vmem, vmem, pl.BlockSpec(memory_space=pltpu.SMEM)] + [vmem] * 7,
        out_specs=[vmem] * len(outs),
        scratch_shapes=scratch,
        compiler_params=pltpu.CompilerParams(
            collective_id=0, has_side_effects=True, vmem_limit_bytes=48 << 20
        ),
        name="line_graph_backward",
    )(
        bond_feats,
        cotangent,
        bond_count,
        src,
        cos,
        w_source,
        w_target,
        w_message,
        w_self,
        gate_angle.reshape(1, cols),
    )
    if fused:
        bond_grad, one, two, four, five, gate = results
        return bond_grad, one, two, four, five, gate.reshape(cols)
    bond_grad, grads, gate = results
    mine = lax.psum_scatter(grads, "dom", scatter_dimension=0, tiled=True)
    gate = lax.psum(gate.reshape(cols), "dom")
    one, four, two, five = (mine[:, i * cols : (i + 1) * cols] for i in range(4))
    return bond_grad, one, two, four, five, gate


def solution(mesh):
    return jax.shard_map(
        functools.partial(per_device, mesh.shape["dom"], mesh.shape["wa"]),
        mesh=mesh,
        in_specs=(
            P("dom", None),
            P("dom", "wa"),
            P("dom"),
            P("dom"),
            P("dom"),
            P(None, "wa"),
            P(None, "wa"),
            P(None, "wa"),
            P(None, "wa"),
            P("wa"),
        ),
        out_specs=(
            P("dom", "wa"),
            P("dom", "wa"),
            P("dom", "wa"),
            P("dom", "wa"),
            P("dom", "wa"),
            P("wa"),
        ),
        check_vma=False,
    )
```

time: 400 us -> 32.2 us (0.08)
  waiting for transfers between devices: 248 us -> 0 us
  other arithmetic: 55.8 us -> 0 us
  local copies, waits for them, and re-layouts: 44.7 us -> 9.22 us
  Pallas kernels: 0 us -> 21.2 us
  blocking collectives: 18.2 us -> 0 us
  between operations: 14.9 us -> 1.36 us
  starting transfers between devices: 12 us -> 0 us
  matrix products: 5.11 us -> 0 us
    reduce_scatter x2 -> x0, waiting for transfers between devices: 130 us -> none  [the longest x1 64.8 us: per_device(): lax.psum_scatter(grad_one, 'dom', scatter_dimension=0, tiled=True)]
    unnamed x8 -> x0, waiting for transfers between devices: 114 us -> none
    scatter-add x2 -> x0, other arithmetic: 35 us -> none  [the longest x1 17.9 us: per_device(): dsource = jax.ops.segment_sum(dpre, source, num_segments=ext_rows)]
    gather x2 -> x0, local copies, waits for them, and re-layouts: 21.6 us -> none  [the longest x1 12 us: per_device(): picked_message = jnp.take(proj_message, source, axis=0)]
    pallas_call x0 -> x1, Pallas kernels: none -> 21.2 us  [per_device(): pl.pallas_call(functools.partial(kernel, n_dom, n_wa, fused), out_shape=o...]
    psum x1 -> x0, blocking collectives: 18.2 us -> none  [per_device(): grad_gate = lax.psum(gate_term, 'dom')]
    reduce_sum x4 -> x0, other arithmetic: 12.2 us -> none  [the longest x3 6.32 us: per_bond(): return values.reshape(capacity, ARITY, values.shape[1]).sum(axis=1)]
    reshape x6 -> x4, local copies, waits for them, and re-layouts: 12.6 us -> 0.43 us  [the longest x2 0.21 us: per_device(): src = source.reshape(capacity, ARITY).T]
  transfers between devices with their start and end apart: 9 -> 0, of which waited for: 6 -> 0; matrix products, arithmetic and copies ran while one was open for 3% -> 0% of each run, Pallas kernels for 0% -> 0%
where the time goes in v1:
time: 32.2 us; the launch traced here: 31.7 us
  Pallas kernels  21.2 us (66%)
  local copies, waits for them, and re-layouts  9.22 us (29%)
  between operations  1.36 us (4%)
    pallas_call x1, Pallas kernels, per_device(): pl.pallas_call(functools.partial(kernel, n_dom, n_wa, fused), out_shape=o...  21.2 us
    unnamed x27, local copies, waits for them, and re-layouts  8.79 us

profile of v1, /device:TPU:0, one launch (start us, length us, event | category | flops | bytes accessed | tf_op | source)
XLA Modules:
  0.0 31.7 jit_solution(7750847987008223999)
XLA Ops:
  1.3 0.9 %copy.24.cot_ref = bf16[256,64]{1,0:T(8,128)(2,1)S(1)} copy(bf16[256,64]{0,1:T(8,128)(2,1)} %param.11) | data formatting | bytes 65536 | tf_op args[1]
  2.2 0.0 copy-start.3
  2.2 0.1 copy.25.ws_ref
  2.3 0.6 %copy-done.3 = bf16[256,64]{0,1:T(8,128)(2,1)S(1)} copy-done((bf16[256,64]{0,1:T(8,128)(2,1)S(1)}, bf16[256,64]{0,1:T(8,128)(2,1)}, u32[]{:S(2)}) %copy-start.3) | copy-done | bytes 32792
  2.9 0.1 copy.26.wt_ref
  3.1 0.6 %copy-done.4 = bf16[256,64]{0,1:T(8,128)(2,1)S(1)} copy-done((bf16[256,64]{0,1:T(8,128)(2,1)S(1)}, bf16[256,64]{0,1:T(8,128)(2,1)}, u32[]{:S(2)}) %copy-start.4) | copy-done | bytes 32792
  3.7 0.1 copy.27.wm_ref
  3.8 0.6 %copy-done.5 = bf16[256,64]{0,1:T(8,128)(2,1)S(1)} copy-done((bf16[256,64]{0,1:T(8,128)(2,1)S(1)}, bf16[256,64]{0,1:T(8,128)(2,1)}, u32[]{:S(2)}) %copy-start.5) | copy-done | bytes 32792
  4.5 0.1 copy.28.wf_ref
  4.6 0.6 %copy-done.6 = s32[3072]{0:T(1024)S(1)} copy-done((s32[3072]{0:T(1024)S(1)}, s32[3072]{0:T(1024)}, u32[]{:S(2)}) %copy-start.6) | copy-done | bytes 12312
  5.2 0.1 reshape.24
  5.3 0.0 copy-start.7
  5.3 0.1 copy.22
  5.4 0.6 %copy-done.7 = f32[3072]{0:T(1024)S(1)} copy-done((f32[3072]{0:T(1024)S(1)}, f32[3072]{0:T(1024)}, u32[]{:S(2)}) %copy-start.7) | copy-done | bytes 12312
  6.0 0.1 reshape.25
  6.2 0.1 copy.23
  6.2 0.7 %copy-done = bf16[256,256]{1,0:T(8,128)(2,1)S(1)} copy-done((bf16[256,256]{1,0:T(8,128)(2,1)S(1)}, bf16[256,256]{1,0:T(8,128)(2,1)}, u32[]{:S(2)}) %copy-start) | copy-done | bytes 131096
  6.9 21.2 %line_graph_backward.1 = (bf16[256,64]{1,0:T(8,128)(2,1)S(1)}, f32[32,64]{1,0:T(8,128)S(1)}, f32[32,64]{1,0:T(8,128)S(1)}, f32[32,64]{1,0:T(8,128)S(1)}, f32[32,64]{1,0:T(8,128)S(1)}, /*index=5*/f32[1,64]{1,0:T(1,128)S(1)}) custom-call(bf16[256,256]{1,0:T(8,128)(2,1)S(1)} %copy-done, bf16[256,64]{1,0:T(8,128)(2,1)S(1)} %copy.24.cot_ref, ...), custom_call_target="tpu_custom_call" | custom-call | tf_op jit(solution)/shard_map/line_graph_backward/pallas_call | solution.py:376
  28.1 0.7 %copy.29 = bf16[256,64]{0,1:T(8,128)(2,1)} copy(bf16[256,64]{1,0:T(8,128)(2,1)S(1)} %get-tuple-element.24) | data formatting | bytes 65536
  28.8 0.6 %copy.36 = f32[32,64]{1,0:T(8,128)} copy(f32[32,64]{1,0:T(8,128)S(1)} %get-tuple-element.37) | data formatting | bytes 16384
  29.4 0.6 %copy.37 = f32[32,64]{1,0:T(8,128)} copy(f32[32,64]{1,0:T(8,128)S(1)} %get-tuple-element.38) | data formatting | bytes 16384
  30.0 0.6 %copy.38 = f32[32,64]{1,0:T(8,128)} copy(f32[32,64]{1,0:T(8,128)S(1)} %get-tuple-element.39) | data formatting | bytes 16384
  30.6 0.6 %copy.39 = f32[32,64]{1,0:T(8,128)} copy(f32[32,64]{1,0:T(8,128)S(1)} %get-tuple-element.40) | data formatting | bytes 16384
  31.2 0.5 %copy.40 = f32[64]{0:T(128)} copy(f32[64]{0:T(128)S(1)} %bitcast.7) | data formatting | bytes 512
  (8 shorter events, 0.0 us)
Async XLA Ops:
  1.3 0.9 %copy-start.2 = (bf16[256,64]{0,1:T(8,128)(2,1)S(1)}, bf16[256,64]{0,1:T(8,128)(2,1)}, u32[]{:S(2)}) copy-start(bf16[256,64]{0,1:T(8,128)(2,1)} %param.15) | copy-start | bytes 98308
  2.2 0.8 %copy-start.3 = (bf16[256,64]{0,1:T(8,128)(2,1)S(1)}, bf16[256,64]{0,1:T(8,128)(2,1)}, u32[]{:S(2)}) copy-start(bf16[256,64]{0,1:T(8,128)(2,1)} %param.16) | copy-start | bytes 98308
  2.9 0.8 %copy-start.4 = (bf16[256,64]{0,1:T(8,128)(2,1)S(1)}, bf16[256,64]{0,1:T(8,128)(2,1)}, u32[]{:S(2)}) copy-start(bf16[256,64]{0,1:T(8,128)(2,1)} %param.17) | copy-start | bytes 98308
  3.7 0.8 %copy-start.5 = (bf16[256,64]{0,1:T(8,128)(2,1)S(1)}, bf16[256,64]{0,1:T(8,128)(2,1)}, u32[]{:S(2)}) copy-start(bf16[256,64]{0,1:T(8,128)(2,1)} %param.18) | copy-start | bytes 98308
  4.5 0.7 %copy-start.6 = (s32[3072]{0:T(1024)S(1)}, s32[3072]{0:T(1024)}, u32[]{:S(2)}) copy-start(s32[3072]{0:T(1024)} %param.13) | copy-start | bytes 36868
  5.3 0.7 %copy-start.7 = (f32[3072]{0:T(1024)S(1)}, f32[3072]{0:T(1024)}, u32[]{:S(2)}) copy-start(f32[3072]{0:T(1024)} %param.14) | copy-start | bytes 36868
  6.0 0.9 %copy-start = (bf16[256,256]{1,0:T(8,128)(2,1)S(1)}, bf16[256,256]{1,0:T(8,128)(2,1)}, u32[]{:S(2)}) copy-start(bf16[256,256]{1,0:T(8,128)(2,1)} %h_ref.1) | copy-start | bytes 393220
  6.2 0.7 %copy-start.1 = (f32[64]{0:T(128)S(1)}, f32[64]{0:T(128)}, u32[]{:S(2)}) copy-start(f32[64]{0:T(128)} %param.19) | copy-start | bytes 772

commit v2 on v1

--- a/solution.py
+++ b/solution.py
@@ -35,20 +35,56 @@
     return values.astype(jnp.float32).T
 
 
+def slot_major(src, cos, capacity):
+    rows = src.shape[0]
+    c_hi = cos.astype(jnp.bfloat16).astype(jnp.float32)
+    parts = [(src >> 4).astype(jnp.float32), (src & 15).astype(jnp.float32), c_hi, cos - c_hi]
+    a = lax.broadcasted_iota(jnp.int32, (LANES, 4 * LANES), 0)
+    z = lax.broadcasted_iota(jnp.int32, (LANES, 4 * LANES), 1)
+    turn = (8 * ARITY) * (z // LANES)
+    mirror = jnp.where(a == (LANES - 1 + turn - z) % LANES, 1.0, 0.0).astype(jnp.bfloat16)
+    mixed = dot(jnp.concatenate(parts, axis=0).astype(jnp.bfloat16), mirror)
+    packed = jnp.concatenate(
+        [
+            jnp.concatenate(
+                [mixed[i * rows : (i + 1) * rows, m * LANES : (m + 1) * LANES] for m in range(4)], axis=0
+            )
+            for i in range(4)
+        ],
+        axis=1,
+    ).astype(jnp.bfloat16)
+    b = lax.broadcasted_iota(jnp.int32, (capacity, 4 * rows), 0)
+    q = lax.broadcasted_iota(jnp.int32, (capacity, 4 * rows), 1)
+    want = ((b // 8) % 4) * rows + (ARITY * b) // LANES
+    x0 = dot(jnp.where(q == want, 1.0, 0.0).astype(jnp.bfloat16), packed)
+    x1 = dot(jnp.where(q == want + 1, 1.0, 0.0).astype(jnp.bfloat16), packed)
+    bb = lax.broadcasted_iota(jnp.int32, (capacity, LANES), 0)
+    p = lax.broadcasted_iota(jnp.int32, (capacity, LANES), 1)
+    at = (LANES - 1 + 8 * ARITY * ((bb // 8) % 4) - p) % LANES
+    first = at >= (ARITY * bb) % LANES
+    def finish(v0, v1):
+        v = jnp.where(first, v0, v1).reshape(capacity // 8, 8, LANES)
+        v = pltpu.roll(v, 0, 2, stride=ARITY, stride_axis=1).reshape(capacity, LANES)
+        return v.T[LANES - 16 :]
+    s = finish(x0[:, :LANES] * 16.0 + x0[:, LANES:2*LANES], x1[:, :LANES] * 16.0 + x1[:, LANES:2*LANES])
+    c = finish(x0[:, 2*LANES:3*LANES] + x0[:, 3*LANES:], x1[:, 2*LANES:3*LANES] + x1[:, 3*LANES:])
+    return s, c
+
+
 def kernel(
     n_dom,
     n_wa,
     fused,
-    h_ref,
-    cot_ref,
-    count_ref,
-    src_ref,
-    cos_ref,
-    ws_ref,
-    wt_ref,
-    wm_ref,
-    wf_ref,
-    ga_ref,
+    h_hbm,
+    cot_hbm,
+    count_hbm,
+    src_hbm,
+    cos_hbm,
+    ws_hbm,
+    wt_hbm,
+    wm_hbm,
+    wf_hbm,
+    ga_hbm,
     bond_out,
     *refs,
 ):
@@ -79,13 +115,21 @@
         wrecv_sem,
         nsend_sem,
         nrecv_sem,
-    ) = refs[:20]
-    if fused:
-        g_full, gbuf, grecv, gsend_sem, grecv_sem = refs[20:]
+        h_ref,
+        cot_ref,
+        count_ref,
+        src_ref,
+        cosine_ref,
+        ga_ref,
+        cos_ref,
+        in_sem,
+    ) = refs[:28]
+    if fused:
+        g_full, gbuf, grecv, gsend_sem, grecv_sem = refs[28:]
     dom = lax.axis_index("dom")
     wa = lax.axis_index("wa")
     capacity, depth = h_ref.shape
-    cols = cot_ref.shape[1]
+    cols = cot_ref.shape[0]
     up = (lax.rem(dom + 1, n_dom), wa)
     down = (lax.rem(dom + n_dom - 1, n_dom), wa)
     doms = range(1, n_dom) if fused else (1, n_dom - 1)
@@ -99,13 +143,29 @@
         pl.semaphore_signal(
             barrier, inc=1, device_id=(dom, lax.rem(wa + k, n_wa)), device_id_type=MESH
         )
-    weights = jnp.concatenate([ws_ref[...], wm_ref[...], wt_ref[...], wf_ref[...]], axis=1)
-    wcat[...] = weights
-    wcat_t[...] = flipped(weights).astype(jnp.bfloat16)
+    loads = []
+    pairs = [
+        (src_hbm, src_ref),
+        (cos_hbm, cosine_ref),
+        (h_hbm, h_ref),
+        (count_hbm, count_ref),
+        (cot_hbm, cot_ref),
+        (ga_hbm, ga_ref),
+    ]
+    for i, w in enumerate((ws_hbm, wm_hbm, wt_hbm, wf_hbm)):
+        pairs.append((w, wcat_t.at[pl.ds(i * cols, cols), :]))
+    for i, (ours, to) in enumerate(pairs):
+        copy = pltpu.make_async_copy(ours, to, in_sem.at[i])
+        copy.start()
+        loads.append(copy)
+    loads[0].wait()
+    loads[1].wait()
+    sources, cosines = slot_major(src_ref[...], cosine_ref[...], capacity)
+    cos_ref[...] = cosines
     pl.semaphore_wait(barrier, len(doms) + n_wa - 1)
 
     to_up = pltpu.make_async_remote_copy(
-        src_ref=h_ref.at[pl.ds(capacity - GHOST, GHOST), :],
+        src_ref=h_hbm.at[pl.ds(capacity - GHOST, GHOST), :],
         dst_ref=gh.at[pl.ds(0, GHOST), :],
         send_sem=halo_send.at[0],
         recv_sem=halo_recv.at[0],
@@ -113,7 +173,7 @@
         device_id_type=MESH,
     )
     to_down = pltpu.make_async_remote_copy(
-        src_ref=h_ref.at[pl.ds(0, GHOST), :],
+        src_ref=h_hbm.at[pl.ds(0, GHOST), :],
         dst_ref=gh.at[pl.ds(GHOST, GHOST), :],
         send_sem=halo_send.at[1],
         recv_sem=halo_recv.at[1],
@@ -124,23 +184,34 @@
     to_down.start()
 
     ext = capacity + 2 * GHOST
-    row_id = lax.broadcasted_iota(jnp.int32, (ext, capacity), 0)
+    row_id = (
+        lax.broadcasted_iota(jnp.int32, (capacity, capacity), 0)
+        .astype(jnp.float32)
+        .astype(jnp.bfloat16)
+    )
+    one = jnp.ones((), jnp.bfloat16)
+    zero = jnp.zeros((), jnp.bfloat16)
     for j in range(ARITY):
-        s = src_ref[j : j + 1, :]
-        s = jnp.where(
-            s < GHOST, s + capacity, jnp.where(s < capacity + GHOST, s - GHOST, s)
+        s = sources[15 - j : 16 - j, :]
+        after = s >= capacity + GHOST
+        own_row = jnp.where((s < GHOST) | after, 512.0, s - GHOST)
+        side = jnp.where(s < GHOST, s, jnp.where(after, s - capacity, 512.0))
+        here = pl.ds(j * capacity, capacity)
+        hot[:capacity, here] = jnp.where(row_id == own_row.astype(jnp.bfloat16), one, zero)
+        hot[capacity:, here] = jnp.where(
+            row_id[: 2 * GHOST] == side.astype(jnp.bfloat16), one, zero
         )
-        hot[:, j * capacity : (j + 1) * capacity] = jnp.where(
-            row_id == s, 1.0, 0.0
-        ).astype(jnp.bfloat16)
+    for copy in loads[2:]:
+        copy.wait()
     h_t[:, :capacity] = flipped(h_ref[...]).astype(jnp.bfloat16)
+    wcat[...] = flipped(wcat_t[...]).astype(jnp.bfloat16)
     proj = dot_nt(wcat_t[...], h_ref[...])
     lane = lax.broadcasted_iota(jnp.int32, (1, capacity), 1)
     count = count_ref[0]
     live = jnp.where(
         (lane < count - GHOST) | (lane >= capacity - GHOST), 1.0, 0.0
     ).astype(jnp.float32)
-    cot_live = flipped(cot_ref[...]) * live
+    cot_live = cot_ref[...].astype(jnp.float32) * live
     angle = jnp.broadcast_to(ga_ref[...], (LANES, cols)).T
     high, low = split(proj[: 2 * cols])
     table[: 2 * cols, :capacity] = high
@@ -170,7 +241,7 @@
             here = pl.ds(j * capacity + at, LANES)
             p1 = picked[0:cols, here] + picked[2 * cols : 3 * cols, here]
             p4 = picked[cols : 2 * cols, here] + picked[3 * cols :, here]
-            pre = p1 + q2 + cos_ref[j : j + 1, at : at + LANES] * angle
+            pre = p1 + q2 + cos_ref[15 - j : 16 - j, at : at + LANES] * angle
             sig = jax.nn.sigmoid(pre)
             sig_s[:, here] = sig
             picked[cols : 2 * cols, here] = p4
@@ -189,7 +260,7 @@
             dmsg = sig * dnum
             dpre = dmsg * (picked[cols : 2 * cols, here] - agg) * (1.0 - sig)
             dq2 = dq2 + dpre
-            gate_sum = gate_sum + cos_ref[j : j + 1, at : at + LANES] * dpre
+            gate_sum = gate_sum + cos_ref[15 - j : 16 - j, at : at + LANES] * dpre
             dcol[:cols, here] = dpre.astype(jnp.bfloat16)
             dcol[cols:, here] = dmsg.astype(jnp.bfloat16)
         parts_z.append(dz.astype(jnp.bfloat16))
@@ -271,7 +342,7 @@
     total = own_w[mine, :]
     for k in range(n_wa - 1):
         total = total + wrecv[k].astype(jnp.float32)
-    gsend[...] = total[:, capacity:]
+    gsend[...] = total[:, capacity:].astype(jnp.bfloat16)
     ncopies = []
     for i, to in enumerate((up, down)):
         copy = pltpu.make_async_remote_copy(
@@ -304,12 +375,24 @@
     for copy in ncopies:
         copy.wait()
     lane_t = lax.broadcasted_iota(jnp.int32, (cols, LANES), 1)
-    below = pltpu.roll(grecv2[0], LANES - GHOST, 1)
-    above = pltpu.roll(grecv2[1], LANES - GHOST, 1)
+    below = pltpu.roll(grecv2[0].astype(jnp.float32), LANES - GHOST, 1)
+    above = pltpu.roll(grecv2[1].astype(jnp.float32), LANES - GHOST, 1)
     first = own[:, :LANES] + jnp.where(lane_t < GHOST, below, 0.0)
     last = own[:, capacity - LANES :] + jnp.where(lane_t >= LANES - GHOST, above, 0.0)
     result = jnp.concatenate([first, own[:, LANES : capacity - LANES], last], axis=1) if capacity > 2 * LANES else jnp.concatenate([first, last], axis=1)
-    bond_out[...] = result.T.astype(jnp.bfloat16)
+    bond_out[...] = result.astype(jnp.bfloat16)
+
+
+def put_out(*refs):
+    count = len(refs) // 2
+    sem = refs[-1]
+    copies = [
+        pltpu.make_async_copy(refs[i], refs[count + i], sem.at[i]) for i in range(count)
+    ]
+    for copy in copies:
+        copy.start()
+    for copy in copies:
+        copy.wait()
 
 
 def per_device(
@@ -332,11 +415,11 @@
     ext = capacity + 2 * GHOST
     chunk = depth // n_dom
     fused = chunk % 16 == 0
-    src = source.reshape(capacity, ARITY).T
-    cos = cosine.reshape(capacity, ARITY).T
+    src = source.reshape(angles // LANES, LANES)
+    cos = cosine.reshape(angles // LANES, LANES)
     f32, bf16 = jnp.float32, jnp.bfloat16
     vmem = pl.BlockSpec(memory_space=pltpu.VMEM)
-    outs = [jax.ShapeDtypeStruct((capacity, cols), bf16)]
+    outs = [jax.ShapeDtypeStruct((cols, capacity), bf16)]
     if fused:
         outs += [jax.ShapeDtypeStruct((chunk, cols), f32)] * 4
     else:
@@ -356,14 +439,22 @@
         pltpu.VMEM((depth, capacity + LANES), f32),
         pltpu.VMEM((n_wa, cols, capacity + LANES), bf16),
         pltpu.VMEM((n_wa - 1, cols, capacity + LANES), bf16),
-        pltpu.VMEM((cols, LANES), f32),
-        pltpu.VMEM((2, cols, LANES), f32),
+        pltpu.VMEM((cols, LANES), bf16),
+        pltpu.VMEM((2, cols, LANES), bf16),
         dma((2,)),
         dma((2,)),
         dma((n_wa - 1,)),
         dma((n_wa - 1,)),
         dma((2,)),
         dma((2,)),
+        pltpu.VMEM((capacity, depth), bf16),
+        pltpu.VMEM((cols, capacity), bf16),
+        pltpu.SMEM((1,), jnp.int32),
+        pltpu.VMEM((angles // LANES, LANES), jnp.int32),
+        pltpu.VMEM((angles // LANES, LANES), f32),
+        pltpu.VMEM((1, cols), f32),
+        pltpu.VMEM((16, capacity), f32),
+        dma((10,)),
     ]
     if fused:
         scratch += [
@@ -376,33 +467,40 @@
     results = pl.pallas_call(
         functools.partial(kernel, n_dom, n_wa, fused),
         out_shape=outs,
-        in_specs=[vmem, vmem, pl.BlockSpec(memory_space=pltpu.SMEM)] + [vmem] * 7,
+        in_specs=[pl.BlockSpec(memory_space=pltpu.HBM)] * 10,
         out_specs=[vmem] * len(outs),
         scratch_shapes=scratch,
         compiler_params=pltpu.CompilerParams(
-            collective_id=0, has_side_effects=True, vmem_limit_bytes=48 << 20
+            collective_id=0, has_side_effects=True, vmem_limit_bytes=67043328
         ),
         name="line_graph_backward",
     )(
         bond_feats,
-        cotangent,
+        cotangent.T,
         bond_count,
         src,
         cos,
-        w_source,
-        w_target,
-        w_message,
-        w_self,
+        w_source.T,
+        w_target.T,
+        w_message.T,
+        w_self.T,
         gate_angle.reshape(1, cols),
     )
     if fused:
-        bond_grad, one, two, four, five, gate = results
-        return bond_grad, one, two, four, five, gate.reshape(cols)
+        bond_grad, one, two, four, five, gate = pl.pallas_call(
+            put_out,
+            out_shape=outs,
+            in_specs=[vmem] * len(outs),
+            out_specs=[pl.BlockSpec(memory_space=pltpu.HBM)] * len(outs),
+            scratch_shapes=[dma((len(outs),))],
+            name="put_out",
+        )(*results)
+        return bond_grad.T, one, two, four, five, gate.reshape(cols)
     bond_grad, grads, gate = results
     mine = lax.psum_scatter(grads, "dom", scatter_dimension=0, tiled=True)
     gate = lax.psum(gate.reshape(cols), "dom")
     one, four, two, five = (mine[:, i * cols : (i + 1) * cols] for i in range(4))
-    return bond_grad, one, two, four, five, gate
+    return bond_grad.T, one, two, four, five, gate
 
 
 def solution(mesh):

time: 32.2 us -> 24.5 us (0.76)
  local copies, waits for them, and re-layouts: 9.22 us -> 0 us
  Pallas kernels: 21.2 us -> 23 us
    unnamed x27 -> x0, local copies, waits for them, and re-layouts: 8.79 us -> none
    pallas_call x0 -> x1, Pallas kernels: none -> 1.49 us  [per_device(): pl.pallas_call(put_out, out_shape=outs, in_specs=[vmem] * len(outs), out_...]
    reshape x4 -> x0, local copies, waits for them, and re-layouts: 0.43 us -> none  [the longest x2 0.21 us: per_device(): src = source.reshape(capacity, ARITY).T]
    pallas_call x1, Pallas kernels: 21.2 us -> 21.5 us  [per_device(): pl.pallas_call(functools.partial(kernel, n_dom, n_wa, fused), out_shape=o...]
where the time goes in v2:
time: 24.5 us; the launch traced here: 24.3 us
  Pallas kernels  23 us (94%)
  between operations  1.29 us (5%)
    pallas_call x1, Pallas kernels, per_device(): pl.pallas_call(functools.partial(kernel, n_dom, n_wa, fused), out_shape=o...  21.5 us
    pallas_call x1, Pallas kernels, per_device(): pl.pallas_call(put_out, out_shape=outs, in_specs=[vmem] * len(outs), out_...  1.49 us

profile of v2, /device:TPU:0, one launch (start us, length us, event | category | flops | bytes accessed | tf_op | source)
XLA Modules:
  0.0 24.3 jit_solution(18083569621915928003)
XLA Ops:
  1.3 21.5 %line_graph_backward.1 = (bf16[64,256]{1,0:T(8,128)(2,1)}, f32[32,64]{1,0:T(8,128)}, f32[32,64]{1,0:T(8,128)}, f32[32,64]{1,0:T(8,128)}, f32[32,64]{1,0:T(8,128)}, /*index=5*/f32[1,64]{1,0:T(1,128)}) custom-call(bf16[256,256]{1,0:T(8,128)(2,1)} %h_hbm.1, bf16[64,256]{1,0:T(8,128)(2,1)} %bitcast.10, s32[1]{0:T(128)S(6)} %copy.16.count_hbm, ...), custom_call_target="tpu_custom_call" | custom-call | tf_op jit(solution)/shard_map/line_graph_backward/pallas_call | solution.py:467
  22.8 1.5 %put_out.1 = (bf16[64,256]{1,0:T(8,128)(2,1)}, f32[32,64]{1,0:T(8,128)}, f32[32,64]{1,0:T(8,128)}, f32[32,64]{1,0:T(8,128)}, f32[32,64]{1,0:T(8,128)}, /*index=5*/f32[1,64]{1,0:T(1,128)}) custom-call(bf16[64,256]{1,0:T(8,128)(2,1)} %get-tuple-element.18.refs_0_, f32[32,64]{1,0:T(8,128)} %get-tuple-element.19.refs_1_, f32[32,64]{1,0:T(8,128)} %get-tuple-element.20.refs_2_, ...), custom_call_target="tpu_custom_call" | custom-call | tf_op jit(solution)/shard_map/put_out/pallas_call | solution.py:490

commit v3 on v2

--- a/solution.py
+++ b/solution.py
@@ -125,7 +125,17 @@
         in_sem,
     ) = refs[:28]
     if fused:
-        g_full, gbuf, grecv, gsend_sem, grecv_sem = refs[28:]
+        (
+            g_full,
+            gbuf,
+            grecv,
+            gsend_sem,
+            grecv_sem,
+            tbuf,
+            trecv,
+            tsend_sem,
+            trecv_sem,
+        ) = refs[28:]
     dom = lax.axis_index("dom")
     wa = lax.axis_index("wa")
     capacity, depth = h_ref.shape
@@ -140,9 +150,9 @@
             barrier, inc=1, device_id=(lax.rem(dom + k, n_dom), wa), device_id_type=MESH
         )
     for k in range(1, n_wa):
-        pl.semaphore_signal(
-            barrier, inc=1, device_id=(dom, lax.rem(wa + k, n_wa)), device_id_type=MESH
-        )
+        side = lax.rem(wa + k, n_wa)
+        for at in (dom, up[0], down[0]):
+            pl.semaphore_signal(barrier, inc=1, device_id=(at, side), device_id_type=MESH)
     loads = []
     pairs = [
         (src_hbm, src_ref),
@@ -158,11 +168,7 @@
         copy = pltpu.make_async_copy(ours, to, in_sem.at[i])
         copy.start()
         loads.append(copy)
-    loads[0].wait()
-    loads[1].wait()
-    sources, cosines = slot_major(src_ref[...], cosine_ref[...], capacity)
-    cos_ref[...] = cosines
-    pl.semaphore_wait(barrier, len(doms) + n_wa - 1)
+    pl.semaphore_wait(barrier, len(doms) + 3 * (n_wa - 1))
 
     to_up = pltpu.make_async_remote_copy(
         src_ref=h_hbm.at[pl.ds(capacity - GHOST, GHOST), :],
@@ -182,6 +188,11 @@
     )
     to_up.start()
     to_down.start()
+
+    loads[0].wait()
+    loads[1].wait()
+    sources, cosines = slot_major(src_ref[...], cosine_ref[...], capacity)
+    cos_ref[...] = cosines
 
     ext = capacity + 2 * GHOST
     row_id = (
@@ -207,7 +218,7 @@
     wcat[...] = flipped(wcat_t[...]).astype(jnp.bfloat16)
     proj = dot_nt(wcat_t[...], h_ref[...])
     lane = lax.broadcasted_iota(jnp.int32, (1, capacity), 1)
-    count = count_ref[0]
+    count = count_ref[...]
     live = jnp.where(
         (lane < count - GHOST) | (lane >= capacity - GHOST), 1.0, 0.0
     ).astype(jnp.float32)
@@ -266,60 +277,59 @@
         parts_z.append(dz.astype(jnp.bfloat16))
         parts_t.append(dq2.astype(jnp.bfloat16))
 
-    rows = dot_nt(dcol[...], hot[...]).astype(jnp.bfloat16)
+    high, low = split(gate_sum)
+    ones = jnp.ones((16, LANES), jnp.bfloat16)
+    gate_row = (dot_nt(ones, high) + dot_nt(ones, low))[0:1]
+    gcopies = []
+    if fused:
+        tbuf[:, :cols] = gate_row
+        tbuf[:, cols:] = jnp.zeros((1, LANES - cols), jnp.float32)
+        for k in range(1, n_dom):
+            copy = pltpu.make_async_remote_copy(
+                src_ref=tbuf,
+                dst_ref=trecv.at[k - 1],
+                send_sem=tsend_sem.at[k - 1],
+                recv_sem=trecv_sem.at[k - 1],
+                device_id=(lax.rem(dom + k, n_dom), wa),
+                device_id_type=MESH,
+            )
+            copy.start()
+            gcopies.append(copy)
+
+    dghost = dot_nt(dcol[...], hot[capacity:, :]).astype(jnp.bfloat16)
+    whole_g = dot(wcat[:, : 2 * cols], dghost).astype(jnp.bfloat16)
+    whole_g = jnp.concatenate(
+        [whole_g, jnp.zeros((depth, LANES - 2 * GHOST), jnp.bfloat16)], axis=1
+    )
+    for c in range(n_wa):
+        gsend[c] = whole_g[c * cols : (c + 1) * cols]
+    ncopies = []
+    for k in range(n_wa):
+        side = lax.rem(wa + k, n_wa)
+        for i, to in enumerate((up[0], down[0])):
+            copy = pltpu.make_async_remote_copy(
+                src_ref=gsend.at[side],
+                dst_ref=grecv2.at[i, k],
+                send_sem=nsend_sem.at[i, k],
+                recv_sem=nrecv_sem.at[i, k],
+                device_id=(to, side),
+                device_id_type=MESH,
+            )
+            copy.start()
+            ncopies.append(copy)
+
+    rows = dot_nt(dcol[...], hot[:capacity, :]).astype(jnp.bfloat16)
     dcat = jnp.concatenate(
-        [
-            rows[:, :capacity],
-            jnp.concatenate(parts_t, axis=1),
-            jnp.concatenate(parts_z, axis=1),
-        ],
-        axis=0,
-    )
-    dghost = rows[:, capacity:]
-
-    whole = dot(wcat[...], dcat)
-    whole_g = dot(wcat[:, : 2 * cols], dghost)
-    whole_g = jnp.concatenate(
-        [whole_g, jnp.zeros((depth, LANES - 2 * GHOST), jnp.float32)], axis=1
-    )
-    own_w[:, :capacity] = whole
-    own_w[:, capacity:] = whole_g
-    for c in range(n_wa):
-        wbuf[c, :, :capacity] = whole[c * cols : (c + 1) * cols].astype(jnp.bfloat16)
-        wbuf[c, :, capacity:] = whole_g[c * cols : (c + 1) * cols].astype(jnp.bfloat16)
-    wcopies = []
-    for k in range(1, n_wa):
-        to = lax.rem(wa + k, n_wa)
-        copy = pltpu.make_async_remote_copy(
-            src_ref=wbuf.at[to],
-            dst_ref=wrecv.at[k - 1],
-            send_sem=wsend_sem.at[k - 1],
-            recv_sem=wrecv_sem.at[k - 1],
-            device_id=(dom, to),
-            device_id_type=MESH,
-        )
-        copy.start()
-        wcopies.append(copy)
-
+        [rows, jnp.concatenate(parts_t, axis=1), jnp.concatenate(parts_z, axis=1)], axis=0
+    )
     grads = dot_nt(h_t[:, :capacity], dcat)
     grads_g = dot_nt(h_t[:, capacity:], dghost)
     grads = jnp.concatenate([grads[:, : 2 * cols] + grads_g, grads[:, 2 * cols :]], axis=1)
-    high, low = split(gate_sum)
-    ones = jnp.ones((16, LANES), jnp.bfloat16)
-    gate_row = dot_nt(ones, high) + dot_nt(ones, low)
-    gcopies = []
     if fused:
         chunk = depth // n_dom
         g_full[...] = grads
-        row16 = lax.broadcasted_iota(jnp.int32, (16, cols), 0)
-        ghigh = gate_row.astype(jnp.bfloat16).astype(jnp.float32)
-        gate_block = jnp.where(row16 == 0, ghigh, gate_row - ghigh)
-        gate_block = jnp.concatenate(
-            [gate_block, jnp.zeros((16, 4 * cols - cols), jnp.float32)], axis=1
-        ).astype(jnp.bfloat16)
         for i in range(n_dom):
-            gbuf[i, :chunk, :] = grads[i * chunk : (i + 1) * chunk].astype(jnp.bfloat16)
-            gbuf[i, chunk:, :] = gate_block
+            gbuf[i] = grads[i * chunk : (i + 1) * chunk].astype(jnp.bfloat16)
         for k in range(1, n_dom):
             to = lax.rem(dom + k, n_dom)
             copy = pltpu.make_async_remote_copy(
@@ -334,7 +344,25 @@
             gcopies.append(copy)
     else:
         g_out[...] = grads
-        gg_out[...] = gate_row[0:1]
+        gg_out[...] = gate_row
+
+    whole = dot(wcat[...], dcat)
+    own_w[...] = whole
+    for c in range(n_wa):
+        wbuf[c] = whole[c * cols : (c + 1) * cols].astype(jnp.bfloat16)
+    wcopies = []
+    for k in range(1, n_wa):
+        to = lax.rem(wa + k, n_wa)
+        copy = pltpu.make_async_remote_copy(
+            src_ref=wbuf.at[to],
+            dst_ref=wrecv.at[k - 1],
+            send_sem=wsend_sem.at[k - 1],
+            recv_sem=wrecv_sem.at[k - 1],
+            device_id=(dom, to),
+            device_id_type=MESH,
+        )
+        copy.start()
+        wcopies.append(copy)
 
     for copy in wcopies:
         copy.wait()
@@ -342,30 +370,15 @@
     total = own_w[mine, :]
     for k in range(n_wa - 1):
         total = total + wrecv[k].astype(jnp.float32)
-    gsend[...] = total[:, capacity:].astype(jnp.bfloat16)
-    ncopies = []
-    for i, to in enumerate((up, down)):
-        copy = pltpu.make_async_remote_copy(
-            src_ref=gsend,
-            dst_ref=grecv2.at[i],
-            send_sem=nsend_sem.at[i],
-            recv_sem=nrecv_sem.at[i],
-            device_id=to,
-            device_id_type=MESH,
-        )
-        copy.start()
-        ncopies.append(copy)
-
-    own = total[:, :capacity] + cot_live
+    own = total + cot_live
     if fused:
         for copy in gcopies:
             copy.wait()
         acc = g_full[pl.ds(pl.multiple_of(dom * chunk, chunk), chunk), :]
-        gate = gate_row[0:1]
+        gate = gate_row
         for k in range(n_dom - 1):
-            acc = acc + grecv[k, :chunk, :].astype(jnp.float32)
-            pair = grecv[k, chunk:, :cols].astype(jnp.float32)
-            gate = gate + pair[0:1] + pair[1:2]
+            acc = acc + grecv[k].astype(jnp.float32)
+            gate = gate + trecv[k][:, :cols]
         g1_out[...] = acc[:, :cols]
         g4_out[...] = acc[:, cols : 2 * cols]
         g2_out[...] = acc[:, 2 * cols : 3 * cols]
@@ -375,8 +388,13 @@
     for copy in ncopies:
         copy.wait()
     lane_t = lax.broadcasted_iota(jnp.int32, (cols, LANES), 1)
-    below = pltpu.roll(grecv2[0].astype(jnp.float32), LANES - GHOST, 1)
-    above = pltpu.roll(grecv2[1].astype(jnp.float32), LANES - GHOST, 1)
+    below = jnp.zeros((cols, LANES), jnp.float32)
+    above = jnp.zeros((cols, LANES), jnp.float32)
+    for k in range(n_wa):
+        below = below + grecv2[0, k].astype(jnp.float32)
+        above = above + grecv2[1, k].astype(jnp.float32)
+    below = pltpu.roll(below, LANES - GHOST, 1)
+    above = pltpu.roll(above, LANES - GHOST, 1)
     first = own[:, :LANES] + jnp.where(lane_t < GHOST, below, 0.0)
     last = own[:, capacity - LANES :] + jnp.where(lane_t >= LANES - GHOST, above, 0.0)
     result = jnp.concatenate([first, own[:, LANES : capacity - LANES], last], axis=1) if capacity > 2 * LANES else jnp.concatenate([first, last], axis=1)
@@ -436,20 +454,20 @@
         pltpu.VMEM((4 * cols, angles), f32),
         pltpu.VMEM((cols, angles), f32),
         pltpu.VMEM((2 * cols, angles), bf16),
-        pltpu.VMEM((depth, capacity + LANES), f32),
-        pltpu.VMEM((n_wa, cols, capacity + LANES), bf16),
-        pltpu.VMEM((n_wa - 1, cols, capacity + LANES), bf16),
-        pltpu.VMEM((cols, LANES), bf16),
-        pltpu.VMEM((2, cols, LANES), bf16),
+        pltpu.VMEM((depth, capacity), f32),
+        pltpu.VMEM((n_wa, cols, capacity), bf16),
+        pltpu.VMEM((n_wa - 1, cols, capacity), bf16),
+        pltpu.VMEM((n_wa, cols, LANES), bf16),
+        pltpu.VMEM((2, n_wa, cols, LANES), bf16),
         dma((2,)),
         dma((2,)),
         dma((n_wa - 1,)),
         dma((n_wa - 1,)),
-        dma((2,)),
-        dma((2,)),
+        dma((2, n_wa)),
+        dma((2, n_wa)),
         pltpu.VMEM((capacity, depth), bf16),
         pltpu.VMEM((cols, capacity), bf16),
-        pltpu.SMEM((1,), jnp.int32),
+        pltpu.VMEM((1, 1), jnp.int32),
         pltpu.VMEM((angles // LANES, LANES), jnp.int32),
         pltpu.VMEM((angles // LANES, LANES), f32),
         pltpu.VMEM((1, cols), f32),
@@ -459,8 +477,12 @@
     if fused:
         scratch += [
             pltpu.VMEM((depth, 4 * cols), f32),
-            pltpu.VMEM((n_dom, chunk + 16, 4 * cols), bf16),
-            pltpu.VMEM((n_dom - 1, chunk + 16, 4 * cols), bf16),
+            pltpu.VMEM((n_dom, chunk, 4 * cols), bf16),
+            pltpu.VMEM((n_dom - 1, chunk, 4 * cols), bf16),
+            dma((n_dom - 1,)),
+            dma((n_dom - 1,)),
+            pltpu.VMEM((1, LANES), f32),
+            pltpu.VMEM((n_dom - 1, 1, LANES), f32),
             dma((n_dom - 1,)),
             dma((n_dom - 1,)),
         ]
@@ -477,7 +499,7 @@
     )(
         bond_feats,
         cotangent.T,
-        bond_count,
+        bond_count.reshape(1, 1),
         src,
         cos,
         w_source.T,

time: 24.5 us -> 23.5 us (0.959)
  Pallas kernels: 23 us -> 22 us
    pallas_call x1, Pallas kernels: 21.5 us -> 20.5 us  [per_device(): pl.pallas_call(functools.partial(kernel, n_dom, n_wa, fused), out_shape=o...]
where the time goes in v3:
time: 23.5 us; the launch traced here: 23.3 us
  Pallas kernels  22 us (94%)
  between operations  1.29 us (5%)
    pallas_call x1, Pallas kernels, per_device(): pl.pallas_call(functools.partial(kernel, n_dom, n_wa, fused), out_shape=o...  20.5 us
    pallas_call x1, Pallas kernels, per_device(): pl.pallas_call(put_out, out_shape=outs, in_specs=[vmem] * len(outs), out_...  1.49 us

profile of v3, /device:TPU:0, one launch (start us, length us, event | category | flops | bytes accessed | tf_op | source)
XLA Modules:
  0.0 23.3 jit_solution(923371985087094503)
XLA Ops:
  1.3 20.5 %line_graph_backward.1 = (bf16[64,256]{1,0:T(8,128)(2,1)}, f32[32,64]{1,0:T(8,128)}, f32[32,64]{1,0:T(8,128)}, f32[32,64]{1,0:T(8,128)}, f32[32,64]{1,0:T(8,128)}, /*index=5*/f32[1,64]{1,0:T(1,128)}) custom-call(bf16[256,256]{1,0:T(8,128)(2,1)} %h_hbm.1, bf16[64,256]{1,0:T(8,128)(2,1)} %bitcast.12, s32[1,1]{1,0:T(1,128)} %bitcast.11.count_hbm, ...), custom_call_target="tpu_custom_call" | custom-call | tf_op jit(solution)/shard_map/line_graph_backward/pallas_call | solution.py:489
  21.8 1.5 %put_out.1 = (bf16[64,256]{1,0:T(8,128)(2,1)}, f32[32,64]{1,0:T(8,128)}, f32[32,64]{1,0:T(8,128)}, f32[32,64]{1,0:T(8,128)}, f32[32,64]{1,0:T(8,128)}, /*index=5*/f32[1,64]{1,0:T(1,128)}) custom-call(bf16[64,256]{1,0:T(8,128)(2,1)} %get-tuple-element.18.refs_0_, f32[32,64]{1,0:T(8,128)} %get-tuple-element.19.refs_1_, f32[32,64]{1,0:T(8,128)} %get-tuple-element.20.refs_2_, ...), custom_call_target="tpu_custom_call" | custom-call | tf_op jit(solution)/shard_map/put_out/pallas_call | solution.py:512

commit v4 on v3

--- a/solution.py
+++ b/solution.py
@@ -69,6 +69,33 @@
     s = finish(x0[:, :LANES] * 16.0 + x0[:, LANES:2*LANES], x1[:, :LANES] * 16.0 + x1[:, LANES:2*LANES])
     c = finish(x0[:, 2*LANES:3*LANES] + x0[:, 3*LANES:], x1[:, 2*LANES:3*LANES] + x1[:, 3*LANES:])
     return s, c
+
+
+def packed_sides(values):
+    count = LANES // GHOST
+    rows = values.shape[0] // count
+    place = lax.broadcasted_iota(jnp.int32, (rows, LANES), 1) // GHOST
+    sides = []
+    for side in range(2):
+        out = None
+        for q in range(count):
+            piece = values[q * rows : (q + 1) * rows]
+            turn = (GHOST * (q - side)) % LANES
+            piece = pltpu.roll(piece, turn, 1) if turn else piece
+            out = piece if out is None else jnp.where(place == q, piece, out)
+        sides.append(out)
+    return sides
+
+
+def unpacked(values, lane_block):
+    count = LANES // GHOST
+    place = lax.broadcasted_iota(jnp.int32, values.shape, 1) // GHOST
+    pieces = []
+    for q in range(count):
+        turn = (GHOST * (lane_block - q)) % LANES
+        piece = pltpu.roll(values, turn, 1) if turn else values
+        pieces.append(jnp.where(place == lane_block, piece, 0.0))
+    return jnp.concatenate(pieces, axis=0)
 
 
 def kernel(
@@ -218,7 +245,7 @@
     wcat[...] = flipped(wcat_t[...]).astype(jnp.bfloat16)
     proj = dot_nt(wcat_t[...], h_ref[...])
     lane = lax.broadcasted_iota(jnp.int32, (1, capacity), 1)
-    count = count_ref[...]
+    count = count_ref[0]
     live = jnp.where(
         (lane < count - GHOST) | (lane >= capacity - GHOST), 1.0, 0.0
     ).astype(jnp.float32)
@@ -297,18 +324,20 @@
             gcopies.append(copy)
 
     dghost = dot_nt(dcol[...], hot[capacity:, :]).astype(jnp.bfloat16)
-    whole_g = dot(wcat[:, : 2 * cols], dghost).astype(jnp.bfloat16)
+    whole_g = dot(wcat[:, : 2 * cols], dghost)
     whole_g = jnp.concatenate(
-        [whole_g, jnp.zeros((depth, LANES - 2 * GHOST), jnp.bfloat16)], axis=1
+        [whole_g, jnp.zeros((depth, LANES - 2 * GHOST), jnp.float32)], axis=1
     )
     for c in range(n_wa):
-        gsend[c] = whole_g[c * cols : (c + 1) * cols]
+        before, after = packed_sides(whole_g[c * cols : (c + 1) * cols])
+        gsend[0, c] = after.astype(jnp.bfloat16)
+        gsend[1, c] = before.astype(jnp.bfloat16)
     ncopies = []
     for k in range(n_wa):
         side = lax.rem(wa + k, n_wa)
         for i, to in enumerate((up[0], down[0])):
             copy = pltpu.make_async_remote_copy(
-                src_ref=gsend.at[side],
+                src_ref=gsend.at[i, side],
                 dst_ref=grecv2.at[i, k],
                 send_sem=nsend_sem.at[i, k],
                 recv_sem=nrecv_sem.at[i, k],
@@ -387,16 +416,13 @@
 
     for copy in ncopies:
         copy.wait()
-    lane_t = lax.broadcasted_iota(jnp.int32, (cols, LANES), 1)
-    below = jnp.zeros((cols, LANES), jnp.float32)
-    above = jnp.zeros((cols, LANES), jnp.float32)
+    below = jnp.zeros(grecv2.shape[2:], jnp.float32)
+    above = jnp.zeros(grecv2.shape[2:], jnp.float32)
     for k in range(n_wa):
         below = below + grecv2[0, k].astype(jnp.float32)
         above = above + grecv2[1, k].astype(jnp.float32)
-    below = pltpu.roll(below, LANES - GHOST, 1)
-    above = pltpu.roll(above, LANES - GHOST, 1)
-    first = own[:, :LANES] + jnp.where(lane_t < GHOST, below, 0.0)
-    last = own[:, capacity - LANES :] + jnp.where(lane_t >= LANES - GHOST, above, 0.0)
+    first = own[:, :LANES] + unpacked(below, 0)
+    last = own[:, capacity - LANES :] + unpacked(above, LANES // GHOST - 1)
     result = jnp.concatenate([first, own[:, LANES : capacity - LANES], last], axis=1) if capacity > 2 * LANES else jnp.concatenate([first, last], axis=1)
     bond_out[...] = result.astype(jnp.bfloat16)
 
@@ -457,8 +483,8 @@
         pltpu.VMEM((depth, capacity), f32),
         pltpu.VMEM((n_wa, cols, capacity), bf16),
         pltpu.VMEM((n_wa - 1, cols, capacity), bf16),
-        pltpu.VMEM((n_wa, cols, LANES), bf16),
-        pltpu.VMEM((2, n_wa, cols, LANES), bf16),
+        pltpu.VMEM((2, n_wa, cols * GHOST // LANES, LANES), bf16),
+        pltpu.VMEM((2, n_wa, cols * GHOST // LANES, LANES), bf16),
         dma((2,)),
         dma((2,)),
         dma((n_wa - 1,)),
@@ -467,7 +493,7 @@
         dma((2, n_wa)),
         pltpu.VMEM((capacity, depth), bf16),
         pltpu.VMEM((cols, capacity), bf16),
-        pltpu.VMEM((1, 1), jnp.int32),
+        pltpu.SMEM((1,), jnp.int32),
         pltpu.VMEM((angles // LANES, LANES), jnp.int32),
         pltpu.VMEM((angles // LANES, LANES), f32),
         pltpu.VMEM((1, cols), f32),
@@ -493,20 +519,27 @@
         out_specs=[vmem] * len(outs),
         scratch_shapes=scratch,
         compiler_params=pltpu.CompilerParams(
-            collective_id=0, has_side_effects=True, vmem_limit_bytes=67043328
+            collective_id=0, has_side_effects=True, vmem_limit_bytes=48 << 20
         ),
         name="line_graph_backward",
     )(
-        bond_feats,
-        cotangent.T,
-        bond_count.reshape(1, 1),
-        src,
-        cos,
-        w_source.T,
-        w_target.T,
-        w_message.T,
-        w_self.T,
-        gate_angle.reshape(1, cols),
+        *(
+            operand
+            if operand.size == 1
+            else pltpu.with_memory_space_constraint(operand, pltpu.HBM)
+            for operand in (
+                bond_feats,
+                cotangent.T,
+                bond_count,
+                src,
+                cos,
+                w_source.T,
+                w_target.T,
+                w_message.T,
+                w_self.T,
+                gate_angle.reshape(1, cols),
+            )
+        )
     )
     if fused:
         bond_grad, one, two, four, five, gate = pl.pallas_call(
@@ -516,7 +549,7 @@
             out_specs=[pl.BlockSpec(memory_space=pltpu.HBM)] * len(outs),
             scratch_shapes=[dma((len(outs),))],
             name="put_out",
-        )(*results)
+        )(*(pltpu.with_memory_space_constraint(r, pltpu.VMEM) for r in results))
         return bond_grad.T, one, two, four, five, gate.reshape(cols)
     bond_grad, grads, gate = results
     mine = lax.psum_scatter(grads, "dom", scatter_dimension=0, tiled=True)

time: 23.5 us -> 21.8 us (0.928)
  Pallas kernels: 22 us -> 20.3 us
    pallas_call x1, Pallas kernels: 20.5 us -> 19.6 us  [per_device(): pl.pallas_call(functools.partial(kernel, n_dom, n_wa, fused), out_shape=o...]
    pallas_call x1, Pallas kernels: 1.49 us -> 0.69 us  [per_device(): pl.pallas_call(put_out, out_shape=outs, in_specs=[vmem] * len(outs), out_...]
where the time goes in v4:
time: 21.8 us; the launch traced here: 21.6 us
  Pallas kernels  20.3 us (93%)
  between operations  1.29 us (6%)
    pallas_call x1, Pallas kernels, per_device(): pl.pallas_call(functools.partial(kernel, n_dom, n_wa, fused), out_shape=o...  19.6 us
    pallas_call x1, Pallas kernels, per_device(): pl.pallas_call(put_out, out_shape=outs, in_specs=[vmem] * len(outs), out_...  0.69 us

profile of v4, /device:TPU:0, one launch (start us, length us, event | category | flops | bytes accessed | tf_op | source)
XLA Modules:
  0.0 21.6 jit_solution(5815051202427143750)
XLA Ops:
  1.3 19.6 %line_graph_backward.1 = (bf16[64,256]{1,0:T(8,128)(2,1)S(1)}, f32[32,64]{1,0:T(8,128)S(1)}, f32[32,64]{1,0:T(8,128)S(1)}, f32[32,64]{1,0:T(8,128)S(1)}, f32[32,64]{1,0:T(8,128)S(1)}, /*index=5*/f32[1,64]{1,0:T(1,128)S(1)}) custom-call(bf16[256,256]{1,0:T(8,128)(2,1)} %h_hbm.1, bf16[64,256]{1,0:T(8,128)(2,1)} %bitcast.10, s32[1]{0:T(128)S(6)} %copy.16.count_hbm, ...), custom_call_target="tpu_custom_call" | custom-call | tf_op jit(solution)/shard_map/line_graph_backward/pallas_call | solution.py:515
  20.9 0.7 %put_out.1 = (bf16[64,256]{1,0:T(8,128)(2,1)}, f32[32,64]{1,0:T(8,128)}, f32[32,64]{1,0:T(8,128)}, f32[32,64]{1,0:T(8,128)}, f32[32,64]{1,0:T(8,128)}, /*index=5*/f32[1,64]{1,0:T(1,128)}) custom-call(bf16[64,256]{1,0:T(8,128)(2,1)S(1)} %get-tuple-element.18.refs_0_, f32[32,64]{1,0:T(8,128)S(1)} %get-tuple-element.19.refs_1_, ...), custom_call_target="tpu_custom_call" | custom-call | tf_op jit(solution)/shard_map/put_out/pallas_call | solution.py:545

commit v5 on v4

--- a/solution.py
+++ b/solution.py
@@ -69,6 +69,16 @@
     s = finish(x0[:, :LANES] * 16.0 + x0[:, LANES:2*LANES], x1[:, :LANES] * 16.0 + x1[:, LANES:2*LANES])
     c = finish(x0[:, 2*LANES:3*LANES] + x0[:, 3*LANES:], x1[:, 2*LANES:3*LANES] + x1[:, 3*LANES:])
     return s, c
+
+
+def partner(me, k, count):
+    if count & (count - 1):
+        return lax.rem(me + k, count)
+    to = 0
+    for i in range(count.bit_length() - 1):
+        bit = lax.rem(me // (1 << i), 2)
+        to = to + (1 << i) * ((1 - bit) if (k >> i) & 1 else bit)
+    return to
 
 
 def packed_sides(values):
@@ -359,8 +369,8 @@
         g_full[...] = grads
         for i in range(n_dom):
             gbuf[i] = grads[i * chunk : (i + 1) * chunk].astype(jnp.bfloat16)
-        for k in range(1, n_dom):
-            to = lax.rem(dom + k, n_dom)
+        for k in range(n_dom - 1, 0, -1):
+            to = partner(dom, k, n_dom)
             copy = pltpu.make_async_remote_copy(
                 src_ref=gbuf.at[to],
                 dst_ref=grecv.at[k - 1],

time: 21.8 us -> 21.8 us (level)
  no operation moved by 1% of the time
where the time goes in v5:
time: 21.8 us; the launch traced here: 21.6 us
  Pallas kernels  20.3 us (93%)
  between operations  1.29 us (6%)
    pallas_call x1, Pallas kernels, per_device(): pl.pallas_call(functools.partial(kernel, n_dom, n_wa, fused), out_shape=o...  19.6 us
    pallas_call x1, Pallas kernels, per_device(): pl.pallas_call(put_out, out_shape=outs, in_specs=[vmem] * len(outs), out_...  0.69 us

profile of v5, /device:TPU:0, one launch (start us, length us, event | category | flops | bytes accessed | tf_op | source)
XLA Modules:
  0.0 21.6 jit_solution(11376217271873034516)
XLA Ops:
  1.3 19.6 %line_graph_backward.1 = (bf16[64,256]{1,0:T(8,128)(2,1)S(1)}, f32[32,64]{1,0:T(8,128)S(1)}, f32[32,64]{1,0:T(8,128)S(1)}, f32[32,64]{1,0:T(8,128)S(1)}, f32[32,64]{1,0:T(8,128)S(1)}, /*index=5*/f32[1,64]{1,0:T(1,128)S(1)}) custom-call(bf16[256,256]{1,0:T(8,128)(2,1)} %h_hbm.1, bf16[64,256]{1,0:T(8,128)(2,1)} %bitcast.10, s32[1]{0:T(128)S(6)} %copy.16.count_hbm, ...), custom_call_target="tpu_custom_call" | custom-call | tf_op jit(solution)/shard_map/line_graph_backward/pallas_call | solution.py:525
  20.9 0.7 %put_out.1 = (bf16[64,256]{1,0:T(8,128)(2,1)}, f32[32,64]{1,0:T(8,128)}, f32[32,64]{1,0:T(8,128)}, f32[32,64]{1,0:T(8,128)}, f32[32,64]{1,0:T(8,128)}, /*index=5*/f32[1,64]{1,0:T(1,128)}) custom-call(bf16[64,256]{1,0:T(8,128)(2,1)S(1)} %get-tuple-element.18.refs_0_, f32[32,64]{1,0:T(8,128)S(1)} %get-tuple-element.19.refs_1_, ...), custom_call_target="tpu_custom_call" | custom-call | tf_op jit(solution)/shard_map/put_out/pallas_call | solution.py:555
